TPU v7x, 256 devices: a whole 4x4x8 slice. The times are simulated.
256 devices in a mesh: seq: 32 (over x, y, core), head: 8 (over z).
Axes of the slice: x: 4, y: 4, z: 8, core: 2. Of those that a mesh axis runs over, the one named last changes fastest.
Arguments:
- tokens: bfloat16 [32768, 2048], P('seq'), may hold values from -6 to 6
- norm_gain: bfloat16 [2048], replicated, may hold values from 0.099609375 to 1.8984375
- w_qkv: bfloat16 [3, 2048, 2048], P(None, None, 'head'), may hold values from -0.176776695 to 0.176776695
- mem_gate: float32 [16], P('head'), may hold values from -3 to 3
- w_out: bfloat16 [2048, 2048], P('head'), may hold values from -0.1875 to 0.1875
Outputs:
- attended: bfloat16 [32768, 2048], P('seq', 'head')
- memory_state: float32 [32, 16, 128, 128], P('seq', 'head')
All inputs are finite; a program needn't handle non-finite values.
Results may differ from a plain program's by a relative error of at most 0.01.
The roundings to bfloat16 on the way count: a program that leaves them out, or rounds other values in their place, can miss the bound.
Values may be sent and summed in bfloat16 or wider, within the bound.
A program may use at most 64 MiB of HBM per device.

v0:
```python
import jax
import jax.numpy as jnp
from jax import lax
from jax.sharding import PartitionSpec as P

HDIM = 128


def sent_together(arrays, axis, dim, along):
    columns = [a.reshape(*a.shape[:along], -1) for a in arrays]
    both = jnp.concatenate(columns, axis=along)
    result, at, gathered = (lax.all_gather(both, axis, axis=dim, tiled=True), 0, [])
    for a, column in zip(arrays, columns):
        section = result[..., at : at + column.shape[along]]
        gathered.append(section.reshape(*section.shape[:along], *a.shape[along:]))
        at += column.shape[along]
    return tuple(gathered)


def elu_one(values_in):
    return jnp.where(values_in > 0, values_in + 1.0, jnp.exp(jnp.minimum(values_in, 0.0)))


def on_device(tokens, norm_gain, w_qkv, mem_gate, w_out):
    seg_len = tokens.shape[0]
    local_heads = w_qkv.shape[2] // HDIM
    float_tokens = tokens.astype(jnp.float32)
    normed = (
        float_tokens
        * lax.rsqrt(jnp.mean(float_tokens * float_tokens, axis=-1, keepdims=True) + 1e-05)
        * norm_gain.astype(jnp.float32)
    ).astype(jnp.bfloat16)
    projected = jnp.einsum("td,cdh->cth", normed, w_qkv, preferred_element_type=jnp.float32).astype(
        jnp.bfloat16
    )
    queries = projected[0].reshape(seg_len, local_heads, HDIM)
    key_rows = projected[1].reshape(seg_len, local_heads, HDIM)
    value_rows = projected[2].reshape(seg_len, local_heads, HDIM)
    sig_keys = elu_one(key_rows.astype(jnp.float32))
    memory_delta = jnp.einsum("thd,the->hde", sig_keys, value_rows.astype(jnp.float32))
    delta_norm = jnp.sum(sig_keys, axis=0)
    zero_memory = jnp.zeros_like(memory_delta)
    zero_norm = jnp.zeros_like(delta_norm)
    my_index = lax.axis_index("seq")
    pieces = tuple(
        (
            part.astype(jnp.float32)
            for part in sent_together(
                (memory_delta[None].astype(jnp.bfloat16), delta_norm[None].astype(jnp.bfloat16)),
                "seq",
                0,
                3,
            )
        )
    )
    row_count = pieces[0].shape[0]
    keep_rows = (jnp.arange(row_count, dtype=jnp.int32) < my_index).astype(jnp.float32)
    memory_prev = zero_memory + jnp.sum(pieces[0] * keep_rows[:, None, None, None], axis=0)
    norm_prev = zero_norm + jnp.sum(pieces[1] * keep_rows[:, None, None], axis=0)
    inv_sqrt = 1.0 / HDIM**0.5
    scores = (
        jnp.einsum("qhd,khd->hqk", queries, key_rows, preferred_element_type=jnp.float32) * inv_sqrt
    )
    row_ids = lax.broadcasted_iota(jnp.int32, (seg_len, seg_len), 0)
    col_ids = lax.broadcasted_iota(jnp.int32, (seg_len, seg_len), 1)
    scores = jnp.where((col_ids <= row_ids)[None], scores, -1e30)
    weights = jax.nn.softmax(scores, axis=-1).astype(jnp.bfloat16)
    local_out = jnp.einsum("hqk,khd->qhd", weights, value_rows, preferred_element_type=jnp.float32)
    sig_q = elu_one(queries.astype(jnp.float32))
    retrieved = jnp.einsum("thd,hde->the", sig_q, memory_prev)
    normalizer = 1.0 + jnp.einsum("thd,hd->th", sig_q, norm_prev)
    gate_share = jax.nn.sigmoid(mem_gate)[None, :, None]
    mixed_out = (
        gate_share * retrieved / normalizer[..., None] + (1.0 - gate_share) * local_out
    ).astype(jnp.bfloat16)
    mixed_out = mixed_out.reshape(seg_len, local_heads * HDIM)
    weight_cols = lax.all_to_all(w_out, "head", split_axis=1, concat_axis=0, tiled=True)
    attended = jnp.dot(
        lax.all_gather(mixed_out, "head", axis=1, tiled=True),
        weight_cols,
        preferred_element_type=jnp.float32,
    ).astype(jnp.bfloat16)
    memory_state = ((memory_prev + memory_delta) / seg_len)[None]
    return (attended, memory_state)


def solution(mesh):
    placed = (P("seq", None), P(), P(None, None, "head"), P("head"), P("head", None))
    return jax.shard_map(
        on_device,
        mesh=mesh,
        in_specs=placed,
        out_specs=(P("seq", "head"), P("seq", "head", None, None)),
        check_vma=False,
    )
```

profile of v0, /device:TPU:1, one launch (start us, length us, event | category | flops | bytes accessed | tf_op | source)
XLA Modules:
  0.0 170.5 jit_solution(17933472047963940664)
XLA Ops:
  7.2 0.0 copy-start
  7.2 0.0 copy-start.2
  7.2 0.0 all-gather.3.cloned.1.call-start
  7.2 0.0 copy-start.1
  7.2 3.2 %fusion.1 = f32[1024]{0:T(1024)S(1)} fusion(bf16[1024,2048]{1,0:T(8,128)(2,1)} %param.5), kind=kLoop, calls=%fused_computation.3 | loop fusion | flops 6290432 | bytes 4198400 | tf_op jit(solution)/shard_map/reduce_sum | solution.py:30
  10.5 0.0 copy-done.2
  10.5 0.0 copy-done
  10.5 1.1 copy-done.1
  11.6 3.9 %fusion.17 = bf16[3,1024,256]{1,2,0:T(8,128)(2,1)S(1)} fusion(bf16[3,2048,256]{2,1,0:T(8,128)(2,1)S(1)} %copy-done, bf16[1024,2048]{1,0:T(8,128)(2,1)S(1)} %copy-done.1, f32[2048]{0:T(1024)S(1)} %convert_element_type.76, f32[1024]{0:T(1024)S(1)} %add_rsqrt_fusion), kind=kOutput, calls=%fused_computation.30 | convolution fusion | flops 3230400512 | bytes 8925184 | tf_op jit(solution)/shard_map/td,cdh->cth/dot_general | solution.py:33
  15.5 0.0 copy-start.3
  15.5 1.2 fusion.58
  16.7 0.4 fusion.32
  17.0 2.1 %copy.44 = bf16[1024,2,128]{2,0,1:T(8,128)(2,1)} copy(bf16[1024,2,128]{0,2,1:T(8,128)(2,1)} %bitcast.59) | data formatting | bytes 1048576 | tf_op jit(solution)/shard_map/reshape;squeeze | solution.py:37
  19.1 1.6 fusion.27
  20.8 0.7 copy.46
  21.4 0.0 all-gather.3.cloned.1.call-update
  21.5 0.2 all-gather.5.cloned.1.call-start
  21.7 2.1 %copy.47 = bf16[1024,2,128]{2,0,1:T(8,128)(2,1)} copy(bf16[1024,2,128]{0,2,1:T(8,128)(2,1)} %bitcast.61) | data formatting | bytes 1048576 | tf_op jit(solution)/shard_map/reshape;squeeze | solution.py:36
  23.8 1.3 iota_compare_fusion
  25.0 0.0 copy-done.3
  25.1 8.2 %fusion.59 = (f32[2,1024]{1,0:T(2,128)S(1)}, f32[2,1024,1024]{1,2,0:T(8,128)}) fusion(pred[1024,1024]{0,1:T(8,128)(4,1)} %iota_compare_fusion, bf16[1024,2,128]{0,2,1:T(8,128)(2,1)} %bitcast.62, bf16[1024,2,128]{0,2,1:T(8,128)(2,1)} %bitcast.60), kind=kOutput, calls=%fused_computation.78 | convolution fusion | flops 545260544 | bytes 10493952 | tf_op jit(solution)/shard_map/sub | solution.py:67
  33.2 5.3 %fusion.24 = f32[1024,2,128]{0,2,1:T(8,128)} fusion(bf16[1024,2,128]{0,2,1:T(8,128)(2,1)} %bitcast.66, f32[2,1024,1024]{1,2,0:T(8,128)} %get-tuple-element.18, f32[2,1024]{1,0:T(2,128)S(1)} %get-tuple-element.17, f32[2]{0:T(128)S(1)} %get-tuple-element.12), kind=kOutput, calls=%fused_computation.36 | convolution fusion | flops 541327360 | bytes 9969672 | tf_op jit(solution)/shard_map/hqk,khd->qhd/dot_general | solution.py:68
  38.5 36.3 %all-gather.3.cloned.1.call-done = bf16[32,2,128,129]{2,1,3,0:T(2,128)(2,1)} async-done(((bf16[1,2,128,129]{2,1,3,0:T(2,128)(2,1)}), bf16[32,2,128,129]{2,1,3,0:T(2,128)(2,1)}) %all-gather.3.cloned.1.call-update) | async-done | bytes 2113552 | tf_op jit(solution)/shard_map/all_gather | solution.py:12
  74.8 0.8 fusion.48
  75.6 1.4 fusion.36
  77.0 3.9 %multiply_reduce_fusion = f32[2,128,128]{1,0,2:T(2,128)S(1)} fusion(f32[32]{0:T(128)S(1)} %compare_convert_fusion, bf16[32,2,128,129]{2,1,3,0:T(2,128)(2,1)} %all-gather.3.cloned.1.call-done), kind=kLoop, calls=%fused_computation.15 | loop fusion | flops 3112960 | bytes 2228352 | tf_op jit(solution)/shard_map/reduce_sum | solution.py:58
  80.9 2.7 %fusion.25 = bf16[1024,2,128]{0,2,1:T(8,128)(2,1)} fusion(f32[1024,2,128]{0,2,1:T(8,128)} %fusion.24, bf16[1024,2,128]{2,0,1:T(8,128)(2,1)} %copy.47, f32[1024,2]{0,1:T(2,128)S(1)} %fusion.49, f32[2]{0:T(128)S(1)} %get-tuple-element.13, f32[2,128,128]{1,0,2:T(2,128)S(1)} %multiply_reduce_fusion), kind=kOutput, calls=%fused_computation.37 | convolution fusion | flops 69468160 | bytes 2236424 | tf_op jit(solution)/shard_map/thd,hde->the/dot_general | solution.py:70
  83.6 0.0 all-gather.5.cloned.1.call-update
  83.6 2.3 %copy.52 = bf16[256,2048]{0,1:T(8,128)(2,1)} copy(bf16[256,2048]{1,0:T(8,128)(2,1)} %param.9) | data formatting | bytes 2097152 | tf_op args[4]
  85.9 46.3 %all_to_all.19 = bf16[256,8,256]{0,2,1:T(8,128)(2,1)} all-to-all(bf16[256,8,256]{0,2,1:T(8,128)(2,1)} %bitcast.58), channel_id=1, replica_groups=mesh['seq'=32,'head'=8] {'head'}, dimensions={1} | all-to-all | bytes 2097152 | tf_op jit(solution)/shard_map/all_to_all | solution.py:77
  132.2 2.3 %copy.53 = bf16[8,256,256]{2,1,0:T(8,128)(2,1)} copy(bf16[8,256,256]{1,2,0:T(8,128)(2,1)} %bitcast.57) | data formatting | bytes 2097152 | tf_op jit(solution)/shard_map/all_to_all | solution.py:77
  134.6 0.8 copy.55
  135.3 23.8 %all-gather.5.cloned.1.call-done = bf16[1024,2048]{0,1:T(8,128)(2,1)} async-done(((bf16[1024,256]{0,1:T(8,128)(2,1)}), bf16[1024,2048]{0,1:T(8,128)(2,1)}) %all-gather.5.cloned.1.call-update) | async-done | bytes 4194320 | tf_op jit(solution)/shard_map/all_gather | solution.py:79
  159.1 4.6 %convolution_convert_fusion = bf16[1024,256]{1,0:T(8,128)(2,1)} fusion(bf16[1024,2048]{0,1:T(8,128)(2,1)} %all-gather.5.cloned.1.call-done, bf16[2048,256]{1,0:T(8,128)(2,1)} %bitcast.63), kind=kOutput, calls=%fused_computation.38 | convolution fusion | flops 1074003968 | bytes 5767168 | tf_op jit(solution)/shard_map/dot_general | solution.py:78
  (9 shorter events, 0.1 us)
Async XLA Ops:
  7.2 3.3 %copy-start = (bf16[3,2048,256]{2,1,0:T(8,128)(2,1)S(1)}, bf16[3,2048,256]{2,1,0:T(8,128)(2,1)}, u32[]{:S(2)}) copy-start(bf16[3,2048,256]{2,1,0:T(8,128)(2,1)} %param.7) | copy-start | bytes 9437188
  7.2 3.3 %copy-start.2 = (bf16[2048]{0:T(1024)(128)(2,1)S(1)}, bf16[2048]{0:T(1024)(128)(2,1)}, u32[]{:S(2)}) copy-start(bf16[2048]{0:T(1024)(128)(2,1)} %param.6) | copy-start | bytes 12292
  7.2 67.6 %all-gather.3.cloned.1.call-start = ((), (), s32[]{:S(2)}) async-start(), calls=%async_computation.1 | async-start | bytes 2179584 | tf_op jit(solution)/shard_map/all_gather | solution.py:12
  7.2 4.4 %copy-start.1 = (bf16[1024,2048]{1,0:T(8,128)(2,1)S(1)}, bf16[1024,2048]{1,0:T(8,128)(2,1)}, u32[]{:S(2)}) copy-start(bf16[1024,2048]{1,0:T(8,128)(2,1)} %param.5) | copy-start | bytes 12582916
  15.5 9.6 %copy-start.3 = (f32[2]{0:T(128)S(1)}, f32[2]{0:T(128)}, u32[]{:S(2)}) copy-start(f32[2]{0:T(128)} %param.8) | copy-start | bytes 28
  21.5 137.7 %all-gather.5.cloned.1.call-start = ((), (), s32[]{:S(2)}) async-start(), calls=%async_computation.2 | async-start | bytes 4718592 | tf_op jit(solution)/shard_map/all_gather | solution.py:79
Sparse Core Ops, SparseCore 0:
  21.6 53.1 all-gather.2
  83.7 75.3 all-gather.4
where the time goes:
time: 171 us
  waiting for transfers between devices  60.1 us (35%)
  blocking collectives  46.3 us (27%)
  matrix products  27.6 us (16%)
  between operations  14.2 us (8%)
  local copies, waits for them, and re-layouts  12.4 us (7%)
  other arithmetic  9.68 us (6%)
    all_to_all x1, blocking collectives, on_device(): lax.all_to_all(w_out, 'head', split_axis=1, concat_axis=0, tiled=True)  46.3 us
    all_gather x1, waiting for transfers between devices, sent_together(): lax.all_gather(both, axis, axis=dim, tiled=True)  36.3 us
    all_gather x1, waiting for transfers between devices, on_device(): lax.all_gather(mixed_out, 'head', axis=1, tiled=True)  23.8 us
    sub x1, matrix products, on_device(): weights = jax.nn.softmax(scores, axis=-1).astype(jnp.bfloat16)  8.15 us
    dot_general x1, matrix products, on_device(): jnp.einsum('hqk,khd->qhd', weights, value_rows, preferred_element_type=jn...  5.3 us
    dot_general x1, matrix products, on_device(): jnp.dot(lax.all_gather(mixed_out, 'head', axis=1, tiled=True), weight_col...  4.57 us
    unnamed x10, local copies, waits for them, and re-layouts  4.15 us
    reduce_sum x1, other arithmetic, on_device(): jnp.sum(pieces[0] * keep_rows[:, None, None, None], axis=0)  3.93 us
  transfers between devices with their start and end apart: 2, of which 2 were waited for; matrix products, arithmetic and copies ran while one was open for 13% of the time, Pallas kernels for 0%

commit v1 on v0

--- a/solution.py
+++ b/solution.py
@@ -22,6 +22,36 @@
 
 
 def on_device(tokens, norm_gain, w_qkv, mem_gate, w_out):
+
+    def _attach_modes(field):
+        e_now, v_next, x_next = (lax.axis_size("head"), lax.axis_index("head"), field.shape[1])
+        history = [ix * e_now if dev_j == 1 else ix for dev_j, ix in enumerate(field.shape)]
+        o_now = taken_in = field
+        j = 1
+        then = lax.dynamic_update_slice_in_dim(
+            jnp.zeros(history, field.dtype), field, v_next * x_next, axis=1
+        )
+        while j < e_now // 2 + 1:
+            o_now = lax.ppermute(
+                o_now,
+                axis_name="head",
+                perm=[(dev_j, (dev_j + 1) % e_now) for dev_j in range(e_now)],
+            )
+            then = lax.dynamic_update_slice_in_dim(
+                then, o_now, (v_next - j) % e_now * x_next, axis=1
+            )
+            if 2 * j < e_now:
+                taken_in = lax.ppermute(
+                    taken_in,
+                    axis_name="head",
+                    perm=[(dev_j, (dev_j - 1) % e_now) for dev_j in range(e_now)],
+                )
+                then = lax.dynamic_update_slice_in_dim(
+                    then, taken_in, (v_next + j) % e_now * x_next, axis=1
+                )
+            j += 1
+        return then
+
     seg_len = tokens.shape[0]
     local_heads = w_qkv.shape[2] // HDIM
     float_tokens = tokens.astype(jnp.float32)
@@ -76,9 +106,7 @@
     mixed_out = mixed_out.reshape(seg_len, local_heads * HDIM)
     weight_cols = lax.all_to_all(w_out, "head", split_axis=1, concat_axis=0, tiled=True)
     attended = jnp.dot(
-        lax.all_gather(mixed_out, "head", axis=1, tiled=True),
-        weight_cols,
-        preferred_element_type=jnp.float32,
+        _attach_modes(mixed_out), weight_cols, preferred_element_type=jnp.float32
     ).astype(jnp.bfloat16)
     memory_state = ((memory_prev + memory_delta) / seg_len)[None]
     return (attended, memory_state)

time: 171 us -> 150 us (0.88); the launches traced: 171 us -> 148 us
  blocking collectives: 46.3 us -> 0 us
  starting transfers between devices: 0.26 us -> 17.7 us
  local copies, waits for them, and re-layouts: 12.4 us -> 18.7 us
  matrix products: 27.6 us -> 24.5 us
  waiting for transfers between devices: 60.1 us -> 62.7 us
    all_to_all x1 -> x0, blocking collectives: 46.3 us -> none  [on_device(): lax.all_to_all(w_out, 'head', split_axis=1, concat_axis=0, tiled=True)]
    ppermute x0 -> x7, waiting for transfers between devices: none -> 37.7 us  [the longest x4 37.7 us: _attach_modes(): lax.ppermute(o_now, axis_name='head', perm=[(dev_j, (dev_j + 1) % e_now)...]
    all_gather x1 -> x0, waiting for transfers between devices: 23.8 us -> none  [on_device(): lax.all_gather(mixed_out, 'head', axis=1, tiled=True)]
    all_gather x1, waiting for transfers between devices: 36.3 us -> 25 us  [sent_together(): lax.all_gather(both, axis, axis=dim, tiled=True)]
    all_to_all x0 -> x1, starting transfers between devices: none -> 9.01 us  [on_device(): lax.all_to_all(w_out, 'head', split_axis=1, concat_axis=0, tiled=True)]
    ppermute x0 -> x7, starting transfers between devices: none -> 8.63 us  [the longest x3 7.27 us: _attach_modes(): lax.ppermute(taken_in, axis_name='head', perm=[(dev_j, (dev_j - 1) % e_no...]
    dynamic_update_slice x0 -> x8, local copies, waits for them, and re-layouts: none -> 4.49 us  [the longest x4 2.25 us: _attach_modes(): lax.dynamic_update_slice_in_dim(then, o_now, (v_next - j) % e_now * x_nex...]
    dot_general x1, matrix products: 4.57 us -> 2.12 us  [on_device(): jnp.dot(_attach_modes(mixed_out), weight_cols, preferred_element_type=jnp...]
  transfers between devices with their start and end apart: 2 -> 9, of which waited for: 2 -> 5; matrix products, arithmetic and copies ran while one was open for 13% -> 24% of each run, Pallas kernels for 0% -> 0%
where the time goes in v1:
time: 150 us; the launch traced here: 148 us
  waiting for transfers between devices  62.7 us (42%)
  matrix products  24.5 us (16%)
  local copies, waits for them, and re-layouts  18.7 us (12%)
  starting transfers between devices  17.7 us (12%)
  between operations  14.2 us (9%)
  other arithmetic  9.73 us (6%)
    ppermute x4, waiting for transfers between devices, _attach_modes(): lax.ppermute(o_now, axis_name='head', perm=[(dev_j, (dev_j + 1) % e_now)...  37.7 us
    all_gather x1, waiting for transfers between devices, sent_together(): lax.all_gather(both, axis, axis=dim, tiled=True)  25 us
    all_to_all x1, starting transfers between devices, on_device(): lax.all_to_all(w_out, 'head', split_axis=1, concat_axis=0, tiled=True)  9.01 us
    sub x1, matrix products, on_device(): weights = jax.nn.softmax(scores, axis=-1).astype(jnp.bfloat16)  8.17 us
    ppermute x3, starting transfers between devices, _attach_modes(): lax.ppermute(taken_in, axis_name='head', perm=[(dev_j, (dev_j - 1) % e_no...  7.27 us
    unnamed x20, local copies, waits for them, and re-layouts  5.46 us
    dot_general x1, matrix products, on_device(): jnp.einsum('hqk,khd->qhd', weights, value_rows, preferred_element_type=jn...  5.38 us
    reduce_sum x1, other arithmetic, on_device(): jnp.sum(pieces[0] * keep_rows[:, None, None, None], axis=0)  3.93 us
  transfers between devices with their start and end apart: 9, of which 5 were waited for; matrix products, arithmetic and copies ran while one was open for 24% of the time, Pallas kernels for 0%

profile of v1, /device:TPU:1, one launch (start us, length us, event | category | flops | bytes accessed | tf_op | source)
XLA Modules:
  0.0 147.5 jit_solution(1892316061743600234)
XLA Ops:
  7.2 0.0 copy-start
  7.2 0.0 copy-start.7
  7.2 0.0 all-gather.2.cloned.1.call-start
  7.2 0.0 copy-start.1
  7.2 3.2 %fusion.1 = f32[1024]{0:T(1024)S(1)} fusion(bf16[1024,2048]{1,0:T(8,128)(2,1)} %param.5), kind=kLoop, calls=%fused_computation.3 | loop fusion | flops 6290432 | bytes 4198400 | tf_op jit(solution)/shard_map/reduce_sum | solution.py:60
  10.5 0.0 copy-done.7
  10.5 0.0 copy-done
  10.5 1.1 copy-done.1
  11.6 3.9 %fusion.17 = bf16[3,1024,256]{1,2,0:T(8,128)(2,1)S(1)} fusion(bf16[3,2048,256]{2,1,0:T(8,128)(2,1)S(1)} %copy-done, bf16[1024,2048]{1,0:T(8,128)(2,1)S(1)} %copy-done.1, f32[2048]{0:T(1024)S(1)} %convert_element_type.76, f32[1024]{0:T(1024)S(1)} %add_rsqrt_fusion), kind=kOutput, calls=%fused_computation.30 | convolution fusion | flops 3230400512 | bytes 8925184 | tf_op jit(solution)/shard_map/td,cdh->cth/dot_general | solution.py:63
  15.5 1.2 fusion.58
  16.7 0.4 fusion.32
  17.0 2.0 %copy.44 = bf16[1024,2,128]{2,0,1:T(8,128)(2,1)} copy(bf16[1024,2,128]{0,2,1:T(8,128)(2,1)} %bitcast.58) | data formatting | bytes 1048576 | tf_op jit(solution)/shard_map/reshape;squeeze | solution.py:67
  19.0 0.0 copy-start.8
  19.0 1.6 %fusion.27 = f32[2,128,128]{1,2,0:T(8,128)S(1)} fusion(bf16[1024,2,128]{0,2,1:T(8,128)(2,1)} %bitcast.66, bf16[1024,2,128]{2,0,1:T(8,128)(2,1)} %copy.44), kind=kOutput, calls=%fused_computation.40 | convolution fusion | flops 68419584 | bytes 1179648 | tf_op jit(solution)/shard_map/thd,the->hde/dot_general | solution.py:70
  20.7 0.7 copy.46
  21.4 0.0 all-gather.2.cloned.1.call-update
  21.5 2.3 %copy.52 = bf16[256,2048]{0,1:T(8,128)(2,1)} copy(bf16[256,2048]{1,0:T(8,128)(2,1)} %param.9) | data formatting | bytes 2097152 | tf_op args[4]
  23.7 9.0 %all-to-all-start = ((bf16[256,8,256]{0,2,1:T(8,128)(2,1)}), bf16[256,8,256]{0,2,1:T(8,128)(2,1)}, u32[]{:S(2)}, u32[]{:S(2)}) async-start(bf16[256,8,256]{0,2,1:T(8,128)(2,1)} %bitcast.57), calls=%async_computation | async-start | bytes 2097152 | tf_op jit(solution)/shard_map/all_to_all | solution.py:107
  32.7 2.0 %copy.47 = bf16[1024,2,128]{2,0,1:T(8,128)(2,1)} copy(bf16[1024,2,128]{0,2,1:T(8,128)(2,1)} %bitcast.60) | data formatting | bytes 1048576 | tf_op jit(solution)/shard_map/reshape;squeeze | solution.py:66
  34.8 1.3 iota_compare_fusion
  36.1 0.0 copy-done.8
  36.1 8.2 %fusion.59 = (f32[2,1024]{1,0:T(2,128)S(1)}, f32[2,1024,1024]{1,2,0:T(8,128)}) fusion(pred[1024,1024]{0,1:T(8,128)(4,1)} %iota_compare_fusion, bf16[1024,2,128]{0,2,1:T(8,128)(2,1)} %bitcast.61, bf16[1024,2,128]{0,2,1:T(8,128)(2,1)} %bitcast.59), kind=kOutput, calls=%fused_computation.86 | convolution fusion | flops 545260544 | bytes 10493952 | tf_op jit(solution)/shard_map/sub | solution.py:97
  44.3 5.4 %fusion.24 = f32[1024,2,128]{0,2,1:T(8,128)} fusion(bf16[1024,2,128]{0,2,1:T(8,128)(2,1)} %bitcast.67, f32[2,1024,1024]{1,2,0:T(8,128)} %get-tuple-element.18, f32[2,1024]{1,0:T(2,128)S(1)} %get-tuple-element.17, f32[2]{0:T(128)S(1)} %get-tuple-element.12), kind=kOutput, calls=%fused_computation.36 | convolution fusion | flops 541327360 | bytes 9969672 | tf_op jit(solution)/shard_map/hqk,khd->qhd/dot_general | solution.py:98
  49.7 25.0 %all-gather.2.cloned.1.call-done = bf16[32,2,128,129]{2,1,3,0:T(2,128)(2,1)} async-done(((bf16[1,2,128,129]{2,1,3,0:T(2,128)(2,1)}), bf16[32,2,128,129]{2,1,3,0:T(2,128)(2,1)}) %all-gather.2.cloned.1.call-update) | async-done | bytes 2113552 | tf_op jit(solution)/shard_map/all_gather | solution.py:12
  74.7 0.8 fusion.48
  75.6 1.4 fusion.36
  77.0 3.9 %multiply_reduce_fusion = f32[2,128,128]{1,0,2:T(2,128)S(1)} fusion(f32[32]{0:T(128)S(1)} %compare_convert_fusion, bf16[32,2,128,129]{2,1,3,0:T(2,128)(2,1)} %all-gather.2.cloned.1.call-done), kind=kLoop, calls=%fused_computation.15 | loop fusion | flops 3112960 | bytes 2228352 | tf_op jit(solution)/shard_map/reduce_sum | solution.py:88
  80.9 1.9 %fusion.25 = bf16[1024,2,128]{0,2,1:T(8,128)(2,1)S(1)} fusion(f32[1024,2,128]{0,2,1:T(8,128)} %fusion.24, bf16[1024,2,128]{2,0,1:T(8,128)(2,1)} %copy.47, f32[1024,2]{0,1:T(2,128)S(1)} %fusion.49, f32[2]{0:T(128)S(1)} %get-tuple-element.13, f32[2,128,128]{1,0,2:T(2,128)S(1)} %multiply_reduce_fusion), kind=kOutput, calls=%fused_computation.37 | convolution fusion | flops 69468160 | bytes 2236424 | tf_op jit(solution)/shard_map/thd,hde->the/dot_general | solution.py:100
  82.8 0.0 copy-start.5
  82.8 1.4 collective-permute-start
  84.2 1.9 %collective-permute-start.1 = (bf16[1024,256]{0,1:T(8,128)(2,1)S(1)}, bf16[1024,256]{0,1:T(8,128)(2,1)}, u32[]{:S(2)}, u32[]{:S(2)}) collective-permute-start(bf16[1024,256]{0,1:T(8,128)(2,1)S(1)} %bitcast.64), channel_id=1, source_target_pairs={{0,7},{1,0},{2,1},{3,2},{4,3},{5,4},{6,5},{7,6},{8,15},{9,8},{10,9... | collective-permute-start | bytes 1572872 | tf_op jit(solution)/shard_map/ppermute | solution.py:44
  86.0 12.0 %collective-permute-done = bf16[1024,256]{0,1:T(8,128)(2,1)S(1)} collective-permute-done((bf16[1024,256]{0,1:T(8,128)(2,1)S(1)}, bf16[1024,256]{0,1:T(8,128)(2,1)S(1)}, u32[]{:S(2)}, u32[]{:S(2)}) %collective-permute-start) | collective-permute-done | bytes 524320 | tf_op jit(solution)/shard_map/ppermute | solution.py:35
  98.1 0.0 copy-start.3
  98.1 0.8 copy-done.3
  98.8 0.0 collective-permute-start.2
  98.8 0.0 collective-permute-done.1
  98.8 2.7 %collective-permute-start.3 = (bf16[1024,256]{0,1:T(8,128)(2,1)}, bf16[1024,256]{0,1:T(8,128)(2,1)}, u32[]{:S(2)}, u32[]{:S(2)}) collective-permute-start(bf16[1024,256]{0,1:T(8,128)(2,1)} %collective-permute-done.1), channel_id=1, source_target_pairs={{0,7},{1,0},{2,1},{3,2},{4,3},{5,4},{6,5},{7,6},{8,15},{9,8},{10,9... | collective-permute-start | bytes 1572872 | tf_op jit(solution)/shard_map/ppermute | solution.py:44
  101.5 11.3 %collective-permute-done.2 = bf16[1024,256]{0,1:T(8,128)(2,1)} collective-permute-done((bf16[1024,256]{0,1:T(8,128)(2,1)S(1)}, bf16[1024,256]{0,1:T(8,128)(2,1)}, u32[]{:S(2)}, u32[]{:S(2)}) %collective-permute-start.2) | collective-permute-done | bytes 524320 | tf_op jit(solution)/shard_map/ppermute | solution.py:35
  112.9 0.0 copy-done.5
  112.9 0.0 collective-permute-start.4
  112.9 0.0 all-to-all-done
  112.9 2.3 %copy.53 = bf16[8,256,256]{2,1,0:T(8,128)(2,1)} copy(bf16[8,256,256]{1,2,0:T(8,128)(2,1)} %bitcast.16) | data formatting | bytes 2097152 | tf_op jit(solution)/shard_map/all_to_all | solution.py:107
  115.2 0.8 copy.55
  115.9 0.0 copy-start.6
  115.9 0.0 copy-start.4
  115.9 0.5 broadcast_in_dim.16
  116.5 0.5 copy-done.6
  117.0 0.0 copy-start.2
  117.0 0.0 collective-permute-done.3
  117.0 2.7 %collective-permute-start.5 = (bf16[1024,256]{0,1:T(8,128)(2,1)}, bf16[1024,256]{0,1:T(8,128)(2,1)S(1)}, u32[]{:S(2)}, u32[]{:S(2)}) collective-permute-start(bf16[1024,256]{0,1:T(8,128)(2,1)} %collective-permute-done.3), channel_id=1, source_target_pairs={{0,7},{1,0},{2,1},{3,2},{4,3},{5,4},{6,5},{7,6},{8,15},{9,8},{10,9... | collective-permute-start | bytes 1572872 | tf_op jit(solution)/shard_map/ppermute | solution.py:44
  119.8 0.0 copy-done.4
  119.8 6.4 %collective-permute-done.4 = bf16[1024,256]{0,1:T(8,128)(2,1)} collective-permute-done((bf16[1024,256]{0,1:T(8,128)(2,1)}, bf16[1024,256]{0,1:T(8,128)(2,1)}, u32[]{:S(2)}, u32[]{:S(2)}) %collective-permute-start.4) | collective-permute-done | bytes 524320 | tf_op jit(solution)/shard_map/ppermute | solution.py:35
  126.2 0.0 collective-permute-start.6
  126.2 1.1 constant_dynamic-update-slice_fusion.5
  127.3 1.1 constant_dynamic-update-slice_fusion.4
  128.4 1.1 constant_dynamic-update-slice_fusion.3
  129.5 1.1 constant_dynamic-update-slice_fusion.2
  130.5 0.0 collective-permute-done.5
  130.6 7.9 %collective-permute-done.6 = bf16[1024,256]{0,1:T(8,128)(2,1)S(1)} collective-permute-done((bf16[1024,256]{0,1:T(8,128)(2,1)}, bf16[1024,256]{0,1:T(8,128)(2,1)S(1)}, u32[]{:S(2)}, u32[]{:S(2)}) %collective-permute-start.6) | collective-permute-done | bytes 524320 | tf_op jit(solution)/shard_map/ppermute | solution.py:35
  138.5 0.0 copy-done.2
  138.6 2.1 %convolution_convert_fusion = bf16[1024,256]{1,0:T(8,128)(2,1)} fusion(bf16[1024,2048]{0,1:T(8,128)(2,1)S(1)} %constant_dynamic-update-slice_fusion, bf16[2048,256]{1,0:T(8,128)(2,1)S(1)} %bitcast.62), kind=kOutput, calls=%fused_computation.38 | convolution fusion | flops 1074003968 | bytes 5767168 | tf_op jit(solution)/shard_map/dot_general | solution.py:108
  (13 shorter events, 0.2 us)
Async XLA Ops:
  7.2 3.3 %copy-start = (bf16[3,2048,256]{2,1,0:T(8,128)(2,1)S(1)}, bf16[3,2048,256]{2,1,0:T(8,128)(2,1)}, u32[]{:S(2)}) copy-start(bf16[3,2048,256]{2,1,0:T(8,128)(2,1)} %param.7) | copy-start | bytes 9437188
  7.2 3.3 %copy-start.7 = (bf16[2048]{0:T(1024)(128)(2,1)S(1)}, bf16[2048]{0:T(1024)(128)(2,1)}, u32[]{:S(2)}) copy-start(bf16[2048]{0:T(1024)(128)(2,1)} %param.6) | copy-start | bytes 12292
  7.2 67.6 %all-gather.2.cloned.1.call-start = ((), (), s32[]{:S(2)}) async-start(), calls=%async_computation.1 | async-start | bytes 2179584 | tf_op jit(solution)/shard_map/all_gather | solution.py:12
  7.2 4.4 %copy-start.1 = (bf16[1024,2048]{1,0:T(8,128)(2,1)S(1)}, bf16[1024,2048]{1,0:T(8,128)(2,1)}, u32[]{:S(2)}) copy-start(bf16[1024,2048]{1,0:T(8,128)(2,1)} %param.5) | copy-start | bytes 12582916
  19.0 17.1 %copy-start.8 = (f32[2]{0:T(128)S(1)}, f32[2]{0:T(128)}, u32[]{:S(2)}) copy-start(f32[2]{0:T(128)} %param.8) | copy-start | bytes 28
  23.7 89.2 %all-to-all-start = ((bf16[256,8,256]{0,2,1:T(8,128)(2,1)}), bf16[256,8,256]{0,2,1:T(8,128)(2,1)}, u32[]{:S(2)}, u32[]{:S(2)}) async-start(bf16[256,8,256]{0,2,1:T(8,128)(2,1)} %bitcast.57), calls=%async_computation | async-start | bytes 2097152 | tf_op jit(solution)/shard_map/all_to_all | solution.py:107
  82.8 30.1 %copy-start.5 = (bf16[1024,2,128]{0,2,1:T(8,128)(2,1)}, bf16[1024,2,128]{0,2,1:T(8,128)(2,1)S(1)}, u32[]{:S(2)}) copy-start(bf16[1024,2,128]{0,2,1:T(8,128)(2,1)S(1)} %fusion.25) | copy-start | bytes 1572868
  82.8 15.2 %collective-permute-start = (bf16[1024,256]{0,1:T(8,128)(2,1)S(1)}, bf16[1024,256]{0,1:T(8,128)(2,1)S(1)}, u32[]{:S(2)}, u32[]{:S(2)}) collective-permute-start(bf16[1024,256]{0,1:T(8,128)(2,1)S(1)} %bitcast.63), channel_id=1, source_target_pairs={{0,1},{1,2},{2,3},{3,4},{4,5},{5,6},{6,7},{7,0},{8,9},{9,10},{10,1... | collective-permute-start | bytes 1572872 | tf_op jit(solution)/shard_map/ppermute | solution.py:35
  84.2 14.7 %collective-permute-start.1 = (bf16[1024,256]{0,1:T(8,128)(2,1)S(1)}, bf16[1024,256]{0,1:T(8,128)(2,1)}, u32[]{:S(2)}, u32[]{:S(2)}) collective-permute-start(bf16[1024,256]{0,1:T(8,128)(2,1)S(1)} %bitcast.64), channel_id=1, source_target_pairs={{0,7},{1,0},{2,1},{3,2},{4,3},{5,4},{6,5},{7,6},{8,15},{9,8},{10,9... | collective-permute-start | bytes 1572872 | tf_op jit(solution)/shard_map/ppermute | solution.py:44
  98.1 0.8 copy-start.3
  98.8 14.0 %collective-permute-start.2 = (bf16[1024,256]{0,1:T(8,128)(2,1)S(1)}, bf16[1024,256]{0,1:T(8,128)(2,1)}, u32[]{:S(2)}, u32[]{:S(2)}) collective-permute-start(bf16[1024,256]{0,1:T(8,128)(2,1)S(1)} %collective-permute-done), channel_id=1, source_target_pairs={{0,1},{1,2},{2,3},{3,4},{4,5},{5,6},{6,7},{7,0},{8,9},{9,10},{10,1... | collective-permute-start | bytes 1572872 | tf_op jit(solution)/shard_map/ppermute | solution.py:35
  98.8 18.2 %collective-permute-start.3 = (bf16[1024,256]{0,1:T(8,128)(2,1)}, bf16[1024,256]{0,1:T(8,128)(2,1)}, u32[]{:S(2)}, u32[]{:S(2)}) collective-permute-start(bf16[1024,256]{0,1:T(8,128)(2,1)} %collective-permute-done.1), channel_id=1, source_target_pairs={{0,7},{1,0},{2,1},{3,2},{4,3},{5,4},{6,5},{7,6},{8,15},{9,8},{10,9... | collective-permute-start | bytes 1572872 | tf_op jit(solution)/shard_map/ppermute | solution.py:44
  112.9 13.3 %collective-permute-start.4 = (bf16[1024,256]{0,1:T(8,128)(2,1)}, bf16[1024,256]{0,1:T(8,128)(2,1)}, u32[]{:S(2)}, u32[]{:S(2)}) collective-permute-start(bf16[1024,256]{0,1:T(8,128)(2,1)} %collective-permute-done.2), channel_id=1, source_target_pairs={{0,1},{1,2},{2,3},{3,4},{4,5},{5,6},{6,7},{7,0},{8,9},{9,10},{10,1... | collective-permute-start | bytes 1572872 | tf_op jit(solution)/shard_map/ppermute | solution.py:35
  115.9 1.0 copy-start.6
  115.9 3.8 %copy-start.4 = (bf16[1024,256]{0,1:T(8,128)(2,1)S(1)}, bf16[1024,256]{0,1:T(8,128)(2,1)}, u32[]{:S(2)}) copy-start(bf16[1024,256]{0,1:T(8,128)(2,1)} %copy-done.3) | copy-start | bytes 1572868
  117.0 21.6 %copy-start.2 = (bf16[8,256,256]{2,1,0:T(8,128)(2,1)S(1)}, bf16[8,256,256]{2,1,0:T(8,128)(2,1)}, u32[]{:S(2)}) copy-start(bf16[8,256,256]{2,1,0:T(8,128)(2,1)} %copy.53) | copy-start | bytes 3145732
  117.0 13.5 %collective-permute-start.5 = (bf16[1024,256]{0,1:T(8,128)(2,1)}, bf16[1024,256]{0,1:T(8,128)(2,1)S(1)}, u32[]{:S(2)}, u32[]{:S(2)}) collective-permute-start(bf16[1024,256]{0,1:T(8,128)(2,1)} %collective-permute-done.3), channel_id=1, source_target_pairs={{0,7},{1,0},{2,1},{3,2},{4,3},{5,4},{6,5},{7,6},{8,15},{9,8},{10,9... | collective-permute-start | bytes 1572872 | tf_op jit(solution)/shard_map/ppermute | solution.py:44
  126.2 12.3 %collective-permute-start.6 = (bf16[1024,256]{0,1:T(8,128)(2,1)}, bf16[1024,256]{0,1:T(8,128)(2,1)S(1)}, u32[]{:S(2)}, u32[]{:S(2)}) collective-permute-start(bf16[1024,256]{0,1:T(8,128)(2,1)} %collective-permute-done.4), channel_id=1, source_target_pairs={{0,1},{1,2},{2,3},{3,4},{4,5},{5,6},{6,7},{7,0},{8,9},{9,10},{10,1... | collective-permute-start | bytes 1572872 | tf_op jit(solution)/shard_map/ppermute | solution.py:35
Sparse Core Ops, SparseCore 0:
  21.6 53.1 all-gather.1
